TPU v7x, 128 devices: a whole 4x4x4 slice. The times are simulated.
128 devices in a mesh: member: 8 (over x, z_hi), space: 16 (over y, z_lo, core).
Axes of the slice: x: 4, y: 4, z: 4 (z_hi: 2, z_lo: 2; z = z_hi * 2 + z_lo), core: 2. Of those that a mesh axis runs over, the one named last changes fastest.
Arguments:
- prior_samples: float32 [256, 128, 4096], P('member', 'space'), may hold values from -6 to 6
- external_drive: float32 [128, 4096], P('space'), may hold values from -6 to 6
- obs_value: float32 [16, 32, 1024], P('space', 'member'), may hold values from -6 to 6
- obs_index: int32 [16, 32, 1024], P('space', 'member'), may hold values from 0 to 1023
- obs_weight: bfloat16 [16, 32, 1024], P('space', 'member'), may hold values from 0.5 to 8
Outputs:
- analysis: float32 [256, 128, 4096], P('member', 'space')
Inputs may be any that keep to these rules, and one draw needn't show every extreme that they name: `obs_index`: the cell is numbered row by row within the region: row times 128 plus column.
All inputs are finite; a program needn't handle non-finite values.
Results may differ from a plain program's by a relative error of at most 0.0017.
Values may be sent and summed in bfloat16 or wider, within the bound.
No kernel may reach another device: no remote copies, remote signals or barrier semaphores. Data moves between devices by JAX's collectives and lax.ppermute only.
A program may use at most 128 MiB of HBM per device.

v0:
```python
import math
from functools import partial

import jax
import jax.numpy as jnp
from jax import lax
from jax.experimental import pallas as pl
from jax.experimental.pallas import tpu as pltpu
from jax.sharding import Mesh, PartitionSpec as P


STEPS = 8
ITERS = 6
ROWS = 8
LANES = 128
PLANE = 4
F32 = jnp.float32
BF16 = jnp.bfloat16


def lane_index(rows):
    return lax.broadcasted_iota(jnp.int32, (rows, LANES), 1)


def halves(x):
    high = x.astype(BF16)
    return high, (x - high.astype(F32)).astype(BF16)


def thirds(x):
    high = x.astype(BF16)
    rest = x - high.astype(F32)
    mid = rest.astype(BF16)
    return high, mid, (rest - mid.astype(F32)).astype(BF16)


def product(a, b):
    ah, al = halves(a)
    bh, bl = halves(b)
    return jnp.dot(
        jnp.concatenate([ah, ah, al], 1),
        jnp.concatenate([bh, bl, bh], 0),
        preferred_element_type=F32,
    )


def against_rows(a, b):
    return lax.dot_general(a, b, (((1,), (1,)), ((), ())), preferred_element_type=F32)


def to_tile(line):
    return jnp.concatenate([line[:, r * LANES : (r + 1) * LANES] for r in range(ROWS)], 0)


def to_line(tile):
    return jnp.concatenate([tile[r : r + 1] for r in range(ROWS)], 1)


def pack_kernel(tiles, prior, chunk, stage):
    lane = lane_index(16)
    groups = tiles // PLANE

    def place(tile):
        return lax.rem(tile, PLANE) * groups + tile // PLANE

    def rounding(tile, carry):
        cols = pl.ds(pl.multiple_of(tile * LANES, LANES), LANES)
        left = [jnp.zeros((16, LANES), F32)] * 2
        slot = lax.rem(tile, 4)
        stage[slot] = prior[:, cols]
        for row in range(ROWS):
            cells = jnp.concatenate(
                [stage[slot, pl.ds(row, 8, stride=8)], stage[slot, pl.ds(64 + row, 8, stride=8)]], 0
            )
            wanted = cells + left[row % 2]
            kept = wanted.astype(BF16)
            left[row % 2] = wanted - kept.astype(F32)
            chunk[place(tile), row] = kept
        return carry

    lax.fori_loop(0, tiles, rounding, 0, unroll=4)

    def edges(tile, carry):
        before = place(lax.rem(tile + tiles - 1, tiles))
        after = place(lax.rem(tile + 1, tiles))
        total = jnp.zeros((16, LANES), F32)
        for row in range(ROWS):
            both = jnp.where(
                lane >= LANES // 2, chunk[before, row].astype(F32), chunk[after, row].astype(F32)
            )
            moved = pltpu.roll(both, (16 * row + 8) % LANES, 1)
            total = jnp.where(lane // 16 == row, moved, total)
        chunk[place(tile), ROWS] = total.astype(BF16)
        return carry

    lax.fori_loop(0, tiles, edges, 0, unroll=4)


def extra_kernel(tiles, me_ref, drive, value, index, weight, extra):
    lane8 = lane_index(8)
    weights = weight[0].astype(F32)
    slot4 = lax.broadcasted_iota(jnp.int32, weights.shape, 0)
    for ahead in range(PLANE):
        part = lax.rem(me_ref[1] + ahead, PLANE)
        tile = me_ref[0] * PLANE + part

        def forcing(t):
            return drive[:, pl.ds(pl.multiple_of(lax.rem(t + tiles, tiles) * LANES, LANES), LANES)]

        main = forcing(tile)
        both = jnp.where(lane8 >= LANES // 2, forcing(tile - 1), forcing(tile + 1))
        chosen = slot4 == part
        for slot, field in ((0, value[0]), (1, index[0].astype(F32)), (2, weights)):
            line = jnp.sum(jnp.where(chosen, field, 0.0), axis=0, keepdims=True)
            extra[ahead, slot : slot + 1, :] = line
        extra[ahead, 5:8, :] = jnp.zeros((3, ROWS * LANES), F32)
        for slot, field in ((3, main), (4, both)):
            for row in range(ROWS):
                extra[ahead, slot : slot + 1, row * LANES : (row + 1) * LANES] = field[row : row + 1]


def pack_extra(me, cols, drive, value, index, weight):
    return pl.pallas_call(
        partial(extra_kernel, cols // LANES),
        in_specs=[pl.BlockSpec(memory_space=pltpu.SMEM)]
        + [pl.BlockSpec(memory_space=pltpu.VMEM)] * 4,
        out_shape=jax.ShapeDtypeStruct((PLANE, 8, ROWS * LANES), F32),
        name="pack_extra",
        compiler_params=pltpu.CompilerParams(vmem_limit_bytes=8 << 20),
    )(me, drive, value, index, weight)


def pack(prior):
    members, rows, cols = prior.shape
    tiles = cols // LANES
    part = members // 2
    return pl.pallas_call(
        partial(pack_kernel, tiles),
        grid=(2,),
        in_specs=[pl.BlockSpec((part * rows, cols), lambda i: (i, 0))],
        out_specs=pl.BlockSpec((tiles, ROWS + 1, part, LANES), lambda i: (0, 0, i, 0)),
        out_shape=jax.ShapeDtypeStruct((tiles, ROWS + 1, members, LANES), BF16),
        scratch_shapes=[pltpu.VMEM((4, part * rows, LANES), F32)],
        name="pack",
    )(prior.reshape(members * rows, cols))


def force_kernel(me_ref, own, one, two, three, extra, force, halo):
    for behind, came in enumerate((own, one, two, three)):
        strip = lax.rem(me_ref[1] + PLANE - behind, PLANE)
        extra[strip] = came[:8]
        halo[strip] = came[8:]
    lane = lane_index(8)
    for strip in range(PLANE + 2):
        if strip == 0:
            source = halo.at[PLANE - 1]
        elif strip == PLANE + 1:
            source = halo.at[0]
        else:
            source = extra.at[strip - 1]
        main = to_tile(source[3:4]) * 0.005
        both = to_tile(source[4:5]) * 0.005
        for b in range(8):
            line = pltpu.roll(main, (LANES + 8 - 32 * (b % 4)) % LANES, 1)
            if b % 4 == 0:
                line = jnp.where(lane < 8, pltpu.roll(both, 8, 1), line)
            if b % 4 == 3:
                line = jnp.where(lane >= 40, pltpu.roll(both, 40, 1), line)
            force[pl.ds(strip * 8 * ROWS + b, 8, stride=8)] = line


def forcing(me, pieces):
    width = pieces[0].shape[1]
    return pl.pallas_call(
        force_kernel,
        in_specs=[pl.BlockSpec(memory_space=pltpu.SMEM)]
        + [pl.BlockSpec(memory_space=pltpu.VMEM)] * PLANE,
        out_shape=[
            jax.ShapeDtypeStruct((PLANE, 8, width), F32),
            jax.ShapeDtypeStruct(((PLANE + 2) * ROWS * 8, LANES), F32),
        ],
        scratch_shapes=[pltpu.VMEM((PLANE, 8, width), F32)],
        name="forcing",
        compiler_params=pltpu.CompilerParams(vmem_limit_bytes=8 << 20),
    )(me, *pieces)


def forecast_kernel(
    inside, cells, top, bottom, force, out, now, later, push, turned, stage, done
):
    depth, span = now.shape[:2]
    lane = lane_index(LANES)
    unit = jnp.where(lax.broadcasted_iota(jnp.int32, lane.shape, 0) == lane, 1.0, 0.0).astype(BF16)
    line = lax.broadcasted_iota(jnp.int32, (8 * span, 2 * LANES), 0)
    sub = lax.rem(line, 8)
    wanted = 32 * lax.rem(sub, 4) + line // 8 - 8
    place = lax.broadcasted_iota(jnp.int32, line.shape, 1)
    spread = (lax.rem(place, LANES) == wanted) & (place // LANES == sub // 4)
    spread = jnp.where(spread, 1.0, 0.0).astype(BF16)

    for strip in range(PLANE + 2):
        if strip == 0:
            source = top
        elif strip == PLANE + 1:
            source = bottom
        else:
            source = cells.at[strip - 1]
        for h in range(2):
            edge = source[4 * h : 4 * h + 4, ROWS].reshape(LANES, LANES)
            turned[0, h * LANES : (h + 1) * LANES] = against_rows(unit, edge) * 0.05

        def load(i, carry):
            for k in range(4):
                r = 4 * i + k
                row = strip * ROWS + r
                both = jnp.concatenate(
                    [source[4 * h : 4 * h + 4, r].reshape(LANES, LANES) for h in range(2)], 1
                )
                main = against_rows(spread, both) * 0.05
                for c in range(span):
                    now[row, c] = main[8 * c : 8 * c + 8]
                at = pl.multiple_of(16 * r, 16)
                for h in range(2):
                    for c in range(8):
                        low = turned[0, pl.ds(h * LANES + at + c, 1)]
                        high = turned[0, pl.ds(h * LANES + at + 8 + c, 1)]
                        now[row, c, 4 * h : 4 * h + 1] = low
                        now[row, span - 8 + c, 4 * h + 3 : 4 * h + 4] = high
                pushes = force[pl.ds(pl.multiple_of(row * 8, 8), 8)]
                for c in range(span):
                    push[row, c] = jnp.broadcast_to(pushes[:, c : c + 1], (8, LANES))
            return carry

        lax.fori_loop(0, ROWS // 4, load, 0)

    keep_top, keep_bottom = inside[0], inside[1]
    source, target = now, later
    for step in range(STEPS):
        low, high = step + 1, span - 2 - step

        def pair(i, carry, source=source, target=target, low=low, high=high):
            row = low + 2 * i
            west = [source[row + k, low - 1] for k in range(2)]
            here = [source[row + k, low] for k in range(2)]
            for c in range(low, high + 1):
                east = [source[row + k, c + 1] for k in range(2)]
                column = [source[row - 1, c], *here, source[row + 2, c]]
                for k in range(2):
                    above, below = column[k], column[k + 2]
                    turn = (west[k] - east[k]) + (above - below) + 0.05
                    target[row + k, c] = (
                        push[row + k, c]
                        + here[k] * turn
                        + 0.05 * (east[k] + west[k])
                        + 0.4 * (above + below)
                    )
                west, here = here, east
            return carry

        lax.fori_loop(0, (depth - 2 - 2 * step) // 2, pair, 0)
        if step < STEPS - 1:
            for c in range(low, high + 1):
                target[ROWS - 1, c] = target[ROWS - 1, c] * keep_top
                target[depth - ROWS, c] = target[depth - ROWS, c] * keep_bottom
        source, target = target, source

    copies = []
    for strip in range(PLANE):

        def save(i, carry):
            for k in range(2):
                row = (strip + 1) * ROWS + 2 * i + k
                for c in range(span - 16):
                    turned[k, 8 * c : 8 * c + 8] = 20.0 * source[row, c + 8]
            for k in range(2):
                at = pl.multiple_of((2 * i + k) * LANES, LANES)
                for h in range(2):
                    columns = [
                        turned[k, pl.ds(64 * c + 4 * h + b, 8, stride=8)]
                        for b in range(4)
                        for c in range(4)
                    ]
                    part = slice(h * LANES, (h + 1) * LANES)
                    stage[strip, part, pl.ds(at, LANES)] = jnp.concatenate(columns, 0).T
            return carry

        lax.fori_loop(0, ROWS // 2, save, 0)
        copies.append(pltpu.make_async_copy(stage.at[strip], out.at[strip], done.at[strip]))
        copies[-1].start()
    for copy in copies:
        copy.wait()


def forecast(inside, cells, top, bottom, force):
    field = pltpu.VMEM(((PLANE + 2) * ROWS, 48, 8, LANES), F32)
    vmem = pl.BlockSpec(memory_space=pltpu.VMEM)
    return pl.pallas_call(
        forecast_kernel,
        in_specs=[pl.BlockSpec(memory_space=pltpu.SMEM), vmem, vmem, vmem, vmem],
        out_specs=pl.BlockSpec(memory_space=pl.ANY),
        out_shape=jax.ShapeDtypeStruct((PLANE, 2 * LANES, ROWS * LANES), F32),
        scratch_shapes=[
            field,
            field,
            field,
            pltpu.VMEM((2, 2 * LANES, LANES), F32),
            pltpu.VMEM((PLANE, 2 * LANES, ROWS * LANES), F32),
            pltpu.SemaphoreType.DMA((PLANE,)),
        ],
        name="forecast",
        compiler_params=pltpu.CompilerParams(vmem_limit_bytes=42 << 20),
    )(inside, cells, top, bottom, force)


def curvature_kernel(pieces, *refs):
    states, (obs, own, up, down) = refs[:pieces], refs[pieces:]
    block = pl.program_id(0)
    blocks = pl.num_programs(0)
    cells = jnp.concatenate([piece[0] for piece in states], 0)
    members = cells.shape[0]
    centre = jnp.sum(cells, axis=0, keepdims=True) * (1.0 / members)
    anomaly = (cells - centre).astype(BF16)
    value, index, weight = obs[0, 0:1], obs[0, 1:2], obs[0, 2:3]
    row_of = jnp.floor(index * (1.0 / LANES))
    col_of = index - row_of * LANES
    count = index.shape[1]
    in_row = lax.broadcasted_iota(jnp.int32, (ROWS, count), 0).astype(F32) == row_of
    in_col = jnp.where(
        lax.broadcasted_iota(jnp.int32, (LANES, count), 0).astype(F32) == col_of, 1.0, 0.0
    ).astype(BF16)
    parts = jnp.concatenate(thirds(to_tile(centre)), 0)
    seen = jnp.dot(parts, in_col, preferred_element_type=F32)
    seen = (seen[:ROWS] + seen[ROWS : 2 * ROWS]) + seen[2 * ROWS :]
    obs_mean = jnp.sum(jnp.where(in_row, seen, 0.0), axis=0, keepdims=True)
    innovation = (value - obs_mean).astype(BF16).astype(F32)
    pull_high, pull_low = halves(weight * innovation)
    spread = jnp.concatenate(
        [
            jnp.where(in_row, weight, 0.0),
            jnp.where(in_row, pull_high.astype(F32), 0.0),
            jnp.where(in_row, pull_low.astype(F32), 0.0),
        ],
        0,
    ).astype(BF16)
    summed = against_rows(spread, in_col)
    weights = summed[:ROWS]
    pulls = summed[ROWS : 2 * ROWS] + summed[2 * ROWS :]
    row_pos = lax.broadcasted_iota(jnp.int32, (ROWS, LANES), 0).astype(F32)
    span = float(ROWS)
    fall_down = jnp.exp(-2.0 * (span - row_pos) * (span - row_pos) / (span * span))
    fall_up = jnp.exp(-2.0 * (row_pos + 1.0) * (row_pos + 1.0) / (span * span))
    wide = anomaly.astype(F32)
    ones = jnp.ones((ROWS, LANES), F32)
    factors = (ones, fall_up, fall_down)
    terms = [
        against_rows((wide * to_line(weights * f)).astype(BF16), anomaly) for f in factors
    ]
    lines = []
    for f in factors:
        lines.extend(thirds(to_line(pulls * f)))
    lines.append(jnp.zeros((7, count), BF16))
    vectors = against_rows(jnp.concatenate(lines, 0), anomaly)
    sides = [
        (vectors[3 * i : 3 * i + 1] + vectors[3 * i + 1 : 3 * i + 2]) + vectors[3 * i + 2 : 3 * i + 3]
        for i in range(3)
    ]
    pad = jnp.zeros((7, members), F32)

    @pl.when(block == 0)
    def _():
        own[...] = jnp.zeros_like(own)
        up[:members] = terms[1]
        up[members:] = jnp.concatenate([sides[1], pad], 0)

    own[block, :members] += terms[0]
    own[block, members:] += jnp.concatenate([sides[0], pad], 0)

    @pl.when(block > 0)
    def _():
        own[block - 1, :members] += terms[1]
        own[block - 1, members:] += jnp.concatenate([sides[1], pad], 0)

    @pl.when(block < blocks - 1)
    def _():
        own[block + 1, :members] += terms[2]
        own[block + 1, members:] += jnp.concatenate([sides[2], pad], 0)

    @pl.when(block == blocks - 1)
    def _():
        down[:members] = terms[2]
        down[members:] = jnp.concatenate([sides[2], pad], 0)


def of_block(states):
    return [pl.BlockSpec((1, *piece.shape[1:]), lambda i: (i, 0, 0)) for piece in states]


def curvatures(states, obs):
    blocks, _, width = states[0].shape
    members = sum(piece.shape[1] for piece in states)
    whole = lambda shape: pl.BlockSpec(shape, lambda i: (0,) * len(shape))
    return pl.pallas_call(
        partial(curvature_kernel, len(states)),
        grid=(blocks,),
        in_specs=[*of_block(states), pl.BlockSpec((1, 8, width), lambda i: (i, 0, 0))],
        out_specs=[
            whole((blocks, members + 8, members)),
            whole((members + 8, members)),
            whole((members + 8, members)),
        ],
        out_shape=[
            jax.ShapeDtypeStruct((blocks, members + 8, members), F32),
            jax.ShapeDtypeStruct((members + 8, members), F32),
            jax.ShapeDtypeStruct((members + 8, members), F32),
        ],
        name="curvature",
        compiler_params=pltpu.CompilerParams(vmem_limit_bytes=16 << 20),
    )(*states, obs)


def transform_kernel(edges, *refs):
    own, *rest = refs
    *halo, out, iterate, inverse = rest
    blocks, size, _ = iterate.shape
    row = lax.broadcasted_iota(jnp.int32, (size, size), 0)
    col = lax.broadcasted_iota(jnp.int32, (size, size), 1)
    diagonal = row == col

    def middle_of(x):
        return jnp.where(diagonal, 1.5 - 0.5 * x, -0.5 * x)

    norms, sides = [], []
    for b in range(blocks):
        place = b * (own.shape[0] - 1) if edges else b + 1
        matrix, side = own[place, :size], own[place, size:]
        if edges:
            matrix, side = matrix + halo[b][:size], side + halo[b][size:]
        matrix = matrix + jnp.where(diagonal, size - 1.0, 0.0)
        squares = jnp.sum(jnp.sum(matrix * matrix, axis=0, keepdims=True), axis=1, keepdims=True)
        norm = jnp.sqrt(squares)
        start = matrix / norm
        middle = middle_of(start)
        inverse[b] = middle
        iterate[b] = product(start, middle)
        norms.append(norm)
        sides.append(side)

    def sweep(i, carry):
        middles = [middle_of(product(inverse[b], iterate[b])) for b in range(blocks)]
        for b in range(blocks):
            both = product(jnp.concatenate([iterate[b], inverse[b]], 0), middles[b])
            iterate[b] = both[:size]
            inverse[b] = both[size:]
        return carry

    lax.fori_loop(0, ITERS - 2, sweep, 0)
    middles = [middle_of(product(inverse[b], iterate[b])) for b in range(blocks)]
    finals = [product(inverse[b], middles[b]) for b in range(blocks)]
    for b in range(blocks):
        flipped = finals[b].T
        inner = product(sides[b], flipped)
        shift = product(inner, flipped) / norms[b]
        out[b, :size] = flipped * (math.sqrt(size - 1.0) / jnp.sqrt(norms[b]))
        out[b, size:] = shift


def transforms(own, *halo):
    total, lines, size = own.shape
    blocks = len(halo) or total - 2
    return pl.pallas_call(
        partial(transform_kernel, bool(halo)),
        out_shape=jax.ShapeDtypeStruct((blocks, lines, size), F32),
        scratch_shapes=[
            pltpu.VMEM((blocks, size, size), F32),
            pltpu.VMEM((blocks, size, size), F32),
        ],
        name="transform",
        compiler_params=pltpu.CompilerParams(vmem_limit_bytes=16 << 20),
    )(own, *halo)


def apply_kernel(share, pieces, *refs):
    states, (inner, outer, out) = refs[:pieces], refs[pieces:]
    block = pl.program_id(0)
    within = (block > 0) & (block < pl.num_programs(0) - 1)
    cells = jnp.concatenate([piece[0] for piece in states], 0)
    members, width = cells.shape
    rows = width // LANES
    weights = jnp.where(within, inner[0], outer[0])
    centre = jnp.sum(cells, axis=0, keepdims=True) * (1.0 / members)
    moved = product(weights, cells - centre)
    common = centre + moved[members : members + 1]
    common_high, common_low = halves(
        jnp.concatenate([common[:, r * LANES : (r + 1) * LANES] for r in range(rows)], 0)
    )
    for part in range(members // share):
        for r in range(rows):
            out[0, part, r * share : (r + 1) * share] = moved[
                part * share : (part + 1) * share, r * LANES : (r + 1) * LANES
            ].astype(BF16)
        out[0, part, rows * share : rows * share + rows] = common_high
        out[0, part, rows * share + rows :] = common_low


def apply_transform(share, begin, rows, states, inner, outer):
    blocks = states[0].shape[0]
    members = sum(piece.shape[1] for piece in states)
    lines = rows * (share + 2)
    return pl.pallas_call(
        partial(apply_kernel, share, len(states)),
        grid=(blocks,),
        in_specs=[
            *[
                pl.BlockSpec((1, piece.shape[1], rows * LANES), lambda i: (i, 0, begin))
                for piece in states
            ],
            pl.BlockSpec(
                (1, members + 8, members), lambda i: (jnp.clip(i - 1, 0, blocks - 3), 0, 0)
            ),
            pl.BlockSpec((1, members + 8, members), lambda i: (i // (blocks - 1), 0, 0)),
        ],
        out_specs=pl.BlockSpec((1, members // share, lines, LANES), lambda i: (i, 0, 0, 0)),
        out_shape=jax.ShapeDtypeStruct((blocks, members // share, lines, LANES), BF16),
        name="apply",
        compiler_params=pltpu.CompilerParams(vmem_limit_bytes=20 << 20),
    )(*states, inner, outer)


def unpack_kernel(share, rows, *refs):
    *chunks, out, stage = refs
    for part in range(PLANE):
        cols = slice(part * LANES, (part + 1) * LANES)
        for half, chunk in enumerate(chunks):
            common = chunk[part, 0, rows * share :].astype(F32)
            common = common[:rows] + common[rows:]
            for r in range(rows):
                field = chunk[part, 0, r * share : (r + 1) * share].astype(F32) + common[r : r + 1]
                for k in range(share // 8):
                    stage[part, pl.ds(64 * k + half * rows + r, 8, stride=8)] = field[
                        8 * k : 8 * k + 8
                    ]
        out[:, cols] = stage[part]


def unpack(share, rows, chunks):
    _, groups, lines, _ = chunks[0].shape
    return pl.pallas_call(
        partial(unpack_kernel, share, rows),
        grid=(groups,),
        in_specs=[pl.BlockSpec((PLANE, 1, lines, LANES), lambda i: (0, i, 0, 0))] * len(chunks),
        out_specs=pl.BlockSpec((share * ROWS, PLANE * LANES), lambda i: (0, i)),
        out_shape=jax.ShapeDtypeStruct((share * ROWS, groups * PLANE * LANES), F32),
        scratch_shapes=[pltpu.VMEM((PLANE, share * ROWS, LANES), F32)],
        name="unpack",
        compiler_params=pltpu.CompilerParams(vmem_limit_bytes=12 << 20),
    )(*chunks)


def local(prior, drive, value, index, weight):
    members, rows, cols = prior.shape
    groups = lax.axis_size("member")
    planes = lax.axis_size("y")
    plane = lax.axis_index("y")
    upward = [(i + 1, i) for i in range(planes - 1)]
    downward = [(i, i + 1) for i in range(planes - 1)]
    me = jnp.stack([lax.axis_index("member"), lax.axis_index("zc")]).astype(jnp.int32)
    inside = jnp.stack([plane > 0, plane < planes - 1]).astype(F32)
    axes = ("zc", "member")
    tied = lax.optimization_barrier
    chunk, drive = tied((pack(prior), drive))
    outward = [
        (PLANE * i + edge, PLANE * j + edge)
        for edge, pairs in ((0, upward), (PLANE - 1, downward))
        for i, j in pairs
    ]
    extra = pack_extra(me, cols, drive, value, index, weight)
    outer_rows = lax.ppermute(extra, ("y", "zc"), outward)
    pieces = [jnp.concatenate([extra[d], outer_rows[d]], 0) for d in range(PLANE)]
    for d in range(1, PLANE):
        pieces[d] = lax.ppermute(
            pieces[d], "zc", [(i, (i + d) % PLANE) for i in range(PLANE)]
        )
    extra, force = forcing(me, pieces)
    chunk = lax.all_to_all(chunk, axes, 0, 0, tiled=True)
    cells = chunk.reshape(PLANE, groups, ROWS + 1, members, LANES)
    bottom = lax.ppermute(cells[0], "y", upward)
    top = lax.ppermute(cells[PLANE - 1], "y", downward)
    states = (forecast(inside, cells, top, bottom, force),)
    own, up, down = curvatures(states, extra)
    from_below = lax.ppermute(up, "y", upward)
    from_above = lax.ppermute(down, "y", downward)
    inner = transforms(own)
    outer = transforms(own, from_above, from_below)
    analysed = apply_transform(members, 0, ROWS, states, inner, outer)
    sent = analysed.reshape(PLANE * groups, *analysed.shape[2:])
    back = lax.all_to_all(sent, axes, 0, 0, tiled=True).reshape(analysed.shape)
    return unpack(members, ROWS, [back]).reshape(members, rows, cols)


def solution(mesh):
    groups, spaces = mesh.devices.shape
    fine = Mesh(mesh.devices.reshape(groups, spaces // PLANE, PLANE), ("member", "y", "zc"))
    rows = ("y", "zc")
    return jax.shard_map(
        local,
        mesh=fine,
        in_specs=(
            P("member", rows, None),
            P(rows, None),
            P(rows, "member", None),
            P(rows, "member", None),
            P(rows, "member", None),
        ),
        out_specs=P("member", rows, None),
        check_vma=False,
    )
```

profile of v0, /device:TPU:1, one launch (start us, length us, event | category | flops | bytes accessed | tf_op | source)
XLA Modules:
  0.0 165.8 jit_solution(6005975559005712297)
XLA Ops:
  0.0 9.4 %pack.1 = bf16[32,9,32,128]{3,2,1,0:T(8,128)(2,1)} custom-call(f32[256,4096]{1,0:T(8,128)} %bitcast.28), custom_call_target="tpu_custom_call" | custom-call | tf_op jit(solution)/shard_map/pack/pallas_call | solution.py:137
  9.4 0.0 copy-start
  9.4 0.0 copy-start.1
  9.4 0.0 copy-start.2
  9.4 0.0 copy-start.3
  9.4 9.6 %all-to-all-start = ((bf16[32,9,32,128]{3,2,1,0:T(8,128)(2,1)}), bf16[32,9,32,128]{3,2,1,0:T(8,128)(2,1)S(1)}, u32[]{:S(2)}, u32[]{:S(2)}) async-start(bf16[32,9,32,128]{3,2,1,0:T(8,128)(2,1)} %pack.1), calls=%async_computation | async-start | bytes 4718592 | tf_op jit(solution)/shard_map/all_to_all | solution.py:584
  18.9 0.1 pad_add_fusion.me_ref
  19.0 0.0 copy-done
  19.0 0.0 copy-done.1
  19.0 0.0 copy-done.2
  19.0 0.0 copy-done.3
  19.0 0.7 pack_extra.1
  19.7 0.7 collective-permute-start.2
  20.4 0.1 add_convert_fusion.inside
  20.5 31.4 %all-to-all-done = bf16[32,9,32,128]{3,2,1,0:T(8,128)(2,1)S(1)} async-done(((bf16[32,9,32,128]{3,2,1,0:T(8,128)(2,1)}), bf16[32,9,32,128]{3,2,1,0:T(8,128)(2,1)S(1)}, u32[]{:S(2)}, u32[]{:S(2)}) %all-to-all-start) | async-done | bytes 2359328 | tf_op jit(solution)/shard_map/all_to_all | solution.py:584
  51.9 0.2 fusion
  52.2 1.3 collective-permute-start.1
  53.5 4.0 %collective-permute-start = (bf16[8,9,32,128]{3,2,1,0:T(8,128)(2,1)S(1)}, bf16[8,9,32,128]{3,2,1,0:T(8,128)(2,1)S(1)}, u32[]{:S(2)}, u32[]{:S(2)}) collective-permute-start(bf16[8,9,32,128]{3,2,1,0:T(8,128)(2,1)S(1)} %get-tuple-element.20), channel_id=1, source_target_pairs={{0,4},{4,8},{8,12},{1,5},{5,9},{9,13},{2,6},{6,10},{10,14},{3,7},{... | collective-permute-start | bytes 1769480 | tf_op jit(solution)/shard_map/ppermute | solution.py:587
  57.5 0.0 collective-permute-done.2
  57.5 0.3 collective-permute-start.3
  57.8 1.6 collective-permute-start.4
  59.5 0.0 collective-permute-start.5
  59.5 0.0 collective-permute-done.3.one
  59.5 3.3 %collective-permute-done.4.two = f32[16,1024]{1,0:T(8,128)S(1)} collective-permute-done((f32[16,1024]{1,0:T(8,128)S(1)}, f32[16,1024]{1,0:T(8,128)S(1)}, u32[]{:S(2)}, u32[]{:S(2)}) %collective-permute-start.4) | collective-permute-done | bytes 65568 | tf_op jit(solution)/shard_map/ppermute | solution.py:580
  62.8 0.7 collective-permute-done.5.three
  63.5 0.7 forcing.1
  64.2 4.7 %collective-permute-done.1.bottom = bf16[8,9,32,128]{3,2,1,0:T(8,128)(2,1)S(1)} collective-permute-done((bf16[8,9,32,128]{3,2,1,0:T(8,128)(2,1)S(1)}, bf16[8,9,32,128]{3,2,1,0:T(8,128)(2,1)S(1)}, u32[]{:S(2)}, u32[]{:S(2)}) %collective-permute-start.1) | collective-permute-done | bytes 589856 | tf_op jit(solution)/shard_map/ppermute | solution.py:586
  69.0 0.9 collective-permute-done.top
  69.9 30.1 %forecast.1.refs_0_ = f32[4,256,1024]{2,1,0:T(8,128)S(1)} custom-call(f32[2]{0:T(128)S(1)} %add_convert_fusion.inside, bf16[4,8,9,32,128]{4,3,2,1,0:T(8,128)(2,1)S(1)} %bitcast.25, bf16[8,9,32,128]{3,2,1,0:T(8,128)(2,1)S(1)} %collective-permute-done.top, bf16[8,9,32,128]{3,2,1,0:T(8,128)(2,1)S(1)} %collective-permute-done.1.bottom, ...), custom_call_target="tpu_custom_call" | custom-call | tf_op jit(solution)/shard_map/forecast/pallas_call | solution.py:297
  99.9 5.1 %curvature.1 = (f32[4,264,256]{2,1,0:T(8,128)S(1)}, f32[264,256]{1,0:T(8,128)S(1)}, f32[264,256]{1,0:T(8,128)S(1)}) custom-call(f32[4,256,1024]{2,1,0:T(8,128)S(1)} %forecast.1.refs_0_, f32[4,8,1024]{2,1,0:T(8,128)S(1)} %get-tuple-element.15.refs_1_), custom_call_target="tpu_custom_call" | custom-call | tf_op jit(solution)/shard_map/curvature/pallas_call | solution.py:402
  105.1 4.1 %collective-permute-start.6 = (f32[264,256]{1,0:T(8,128)S(1)}, f32[264,256]{1,0:T(8,128)S(1)}, u32[]{:S(2)}, u32[]{:S(2)}) collective-permute-start(f32[264,256]{1,0:T(8,128)S(1)} %get-tuple-element.17), channel_id=1, source_target_pairs={{0,4},{4,8},{8,12},{1,5},{5,9},{9,13},{2,6},{6,10},{10,14},{3,7},{... | collective-permute-start | bytes 811016 | tf_op jit(solution)/shard_map/ppermute | solution.py:591
  109.2 1.5 collective-permute-start.7
  110.7 5.7 %transform.2.refs_1_ = f32[2,264,256]{2,1,0:T(8,128)S(1)} custom-call(f32[4,264,256]{2,1,0:T(8,128)S(1)} %get-tuple-element.16.refs_0_), custom_call_target="tpu_custom_call" | custom-call | tf_op jit(solution)/shard_map/transform/pallas_call | solution.py:470
  116.4 0.0 collective-permute-done.6.refs_1_
  116.4 1.3 collective-permute-done.7.refs_2_
  117.7 5.7 %transform.3.refs_2_ = f32[2,264,256]{2,1,0:T(8,128)S(1)} custom-call(f32[4,264,256]{2,1,0:T(8,128)S(1)} %get-tuple-element.16.refs_0_, f32[264,256]{1,0:T(8,128)S(1)} %collective-permute-done.6.refs_1_, f32[264,256]{1,0:T(8,128)S(1)} %collective-permute-done.7.refs_2_), custom_call_target="tpu_custom_call" | custom-call | tf_op jit(solution)/shard_map/transform/pallas_call | solution.py:470
  123.5 2.9 %apply.1 = bf16[4,8,272,128]{3,2,1,0:T(8,128)(2,1)S(1)} custom-call(f32[4,256,1024]{2,1,0:T(8,128)S(1)} %forecast.1.refs_0_, f32[2,264,256]{2,1,0:T(8,128)S(1)} %transform.2.refs_1_, f32[2,264,256]{2,1,0:T(8,128)S(1)} %transform.3.refs_2_), custom_call_target="tpu_custom_call" | custom-call | tf_op jit(solution)/shard_map/apply/pallas_call | solution.py:509
  126.4 35.2 %all_to_all.10 = bf16[32,272,128]{2,1,0:T(8,128)(2,1)S(1)} all-to-all(bf16[32,272,128]{2,1,0:T(8,128)(2,1)S(1)} %bitcast.26), channel_id=1, replica_groups=mesh['member'=8,'y'=4,'zc'=4] {'zc','member'}, dimensions={0} | all-to-all | bytes 4456448 | tf_op jit(solution)/shard_map/all_to_all | solution.py:596
  161.6 4.2 %unpack.1 = f32[256,4096]{1,0:T(8,128)} custom-call(bf16[4,8,272,128]{3,2,1,0:T(8,128)(2,1)S(1)} %bitcast.27), custom_call_target="tpu_custom_call" | custom-call | tf_op jit(solution)/shard_map/unpack/pallas_call | solution.py:547
  (6 shorter events, 0.0 us)
Async XLA Ops:
  9.4 9.7 %copy-start = (f32[8,4096]{1,0:T(8,128)S(1)}, f32[8,4096]{1,0:T(8,128)}, u32[]{:S(2)}) copy-start(f32[8,4096]{1,0:T(8,128)} %drive) | copy-start | bytes 393220
  9.4 9.7 %copy-start.1 = (f32[1,4,1024]{2,1,0:T(4,128)S(1)}, f32[1,4,1024]{2,1,0:T(4,128)}, u32[]{:S(2)}) copy-start(f32[1,4,1024]{2,1,0:T(4,128)} %value.1) | copy-start | bytes 49156
  9.4 9.7 %copy-start.2 = (s32[1,4,1024]{2,1,0:T(4,128)S(1)}, s32[1,4,1024]{2,1,0:T(4,128)}, u32[]{:S(2)}) copy-start(s32[1,4,1024]{2,1,0:T(4,128)} %index.1) | copy-start | bytes 49156
  9.4 9.7 %copy-start.3 = (bf16[1,4,1024]{2,1,0:T(4,128)(2,1)S(1)}, bf16[1,4,1024]{2,1,0:T(4,128)(2,1)}, u32[]{:S(2)}) copy-start(bf16[1,4,1024]{2,1,0:T(4,128)(2,1)} %weight.1) | copy-start | bytes 24580
  9.4 42.6 %all-to-all-start = ((bf16[32,9,32,128]{3,2,1,0:T(8,128)(2,1)}), bf16[32,9,32,128]{3,2,1,0:T(8,128)(2,1)S(1)}, u32[]{:S(2)}, u32[]{:S(2)}) async-start(bf16[32,9,32,128]{3,2,1,0:T(8,128)(2,1)} %pack.1), calls=%async_computation | async-start | bytes 4718592 | tf_op jit(solution)/shard_map/all_to_all | solution.py:584
  19.7 37.7 %collective-permute-start.2 = (f32[4,8,1024]{2,1,0:T(8,128)S(1)}, f32[4,8,1024]{2,1,0:T(8,128)S(1)}, u32[]{:S(2)}, u32[]{:S(2)}) collective-permute-start(f32[4,8,1024]{2,1,0:T(8,128)S(1)} %pack_extra.1), channel_id=1, source_target_pairs={{4,0},{8,4},{12,8},{3,7},{7,11},{11,15},{20,16},{24,20},{28,24},{1... | collective-permute-start | bytes 393224 | tf_op jit(solution)/shard_map/ppermute | solution.py:577
  52.2 16.8 %collective-permute-start.1 = (bf16[8,9,32,128]{3,2,1,0:T(8,128)(2,1)S(1)}, bf16[8,9,32,128]{3,2,1,0:T(8,128)(2,1)S(1)}, u32[]{:S(2)}, u32[]{:S(2)}) collective-permute-start(bf16[8,9,32,128]{3,2,1,0:T(8,128)(2,1)S(1)} %get-tuple-element.19), channel_id=1, source_target_pairs={{4,0},{8,4},{12,8},{5,1},{9,5},{13,9},{6,2},{10,6},{14,10},{7,3},{... | collective-permute-start | bytes 1769480 | tf_op jit(solution)/shard_map/ppermute | solution.py:586
  53.5 16.4 %collective-permute-start = (bf16[8,9,32,128]{3,2,1,0:T(8,128)(2,1)S(1)}, bf16[8,9,32,128]{3,2,1,0:T(8,128)(2,1)S(1)}, u32[]{:S(2)}, u32[]{:S(2)}) collective-permute-start(bf16[8,9,32,128]{3,2,1,0:T(8,128)(2,1)S(1)} %get-tuple-element.20), channel_id=1, source_target_pairs={{0,4},{4,8},{8,12},{1,5},{5,9},{9,13},{2,6},{6,10},{10,14},{3,7},{... | collective-permute-start | bytes 1769480 | tf_op jit(solution)/shard_map/ppermute | solution.py:587
  57.5 2.0 %collective-permute-start.3 = (f32[16,1024]{1,0:T(8,128)S(1)}, f32[16,1024]{1,0:T(8,128)S(1)}, u32[]{:S(2)}, u32[]{:S(2)}) collective-permute-start(f32[16,1024]{1,0:T(8,128)S(1)} %pad_maximum_fusion.1), channel_id=1, source_target_pairs={{0,1},{1,2},{2,3},{3,0},{4,5},{5,6},{6,7},{7,4},{8,9},{9,10},{10,1... | collective-permute-start | bytes 196616 | tf_op jit(solution)/shard_map/ppermute | solution.py:580
  57.8 5.0 %collective-permute-start.4 = (f32[16,1024]{1,0:T(8,128)S(1)}, f32[16,1024]{1,0:T(8,128)S(1)}, u32[]{:S(2)}, u32[]{:S(2)}) collective-permute-start(f32[16,1024]{1,0:T(8,128)S(1)} %pad_maximum_fusion.2), channel_id=1, source_target_pairs={{0,2},{1,3},{2,0},{3,1},{4,6},{5,7},{6,4},{7,5},{8,10},{9,11},{10,... | collective-permute-start | bytes 196616 | tf_op jit(solution)/shard_map/ppermute | solution.py:580
  59.5 4.0 %collective-permute-start.5 = (f32[16,1024]{1,0:T(8,128)S(1)}, f32[16,1024]{1,0:T(8,128)S(1)}, u32[]{:S(2)}, u32[]{:S(2)}) collective-permute-start(f32[16,1024]{1,0:T(8,128)S(1)} %pad_maximum_fusion.3), channel_id=1, source_target_pairs={{0,3},{1,0},{2,1},{3,2},{4,7},{5,4},{6,5},{7,6},{8,11},{9,8},{10,9... | collective-permute-start | bytes 196616 | tf_op jit(solution)/shard_map/ppermute | solution.py:580
  105.1 11.3 %collective-permute-start.6 = (f32[264,256]{1,0:T(8,128)S(1)}, f32[264,256]{1,0:T(8,128)S(1)}, u32[]{:S(2)}, u32[]{:S(2)}) collective-permute-start(f32[264,256]{1,0:T(8,128)S(1)} %get-tuple-element.17), channel_id=1, source_target_pairs={{0,4},{4,8},{8,12},{1,5},{5,9},{9,13},{2,6},{6,10},{10,14},{3,7},{... | collective-permute-start | bytes 811016 | tf_op jit(solution)/shard_map/ppermute | solution.py:591
  109.2 8.5 %collective-permute-start.7 = (f32[264,256]{1,0:T(8,128)S(1)}, f32[264,256]{1,0:T(8,128)S(1)}, u32[]{:S(2)}, u32[]{:S(2)}) collective-permute-start(f32[264,256]{1,0:T(8,128)S(1)} %get-tuple-element.18), channel_id=1, source_target_pairs={{4,0},{8,4},{12,8},{5,1},{9,5},{13,9},{6,2},{10,6},{14,10},{7,3},{... | collective-permute-start | bytes 811016 | tf_op jit(solution)/shard_map/ppermute | solution.py:590
where the time goes:
time: 166 us
  Pallas kernels  64.5 us (39%)
  waiting for transfers between devices  42.4 us (26%)
  blocking collectives  35.2 us (21%)
  starting transfers between devices  23.1 us (14%)
    all_to_all x1, blocking collectives, local(): back = lax.all_to_all(sent, axes, 0, 0, tiled=True).reshape(analysed.shape)  35.2 us
    all_to_all x1, waiting for transfers between devices, local(): chunk = lax.all_to_all(chunk, axes, 0, 0, tiled=True)  31.4 us
    pallas_call x1, Pallas kernels, forecast(): pl.pallas_call(forecast_kernel, in_specs=[pl.BlockSpec(memory_space=pltpu...  30.1 us
    pallas_call x2, Pallas kernels, transforms(): pl.pallas_call(partial(transform_kernel, bool(halo)), out_shape=jax.Shape...  11.4 us
    all_to_all x1, starting transfers between devices, local(): chunk = lax.all_to_all(chunk, axes, 0, 0, tiled=True)  9.57 us
    pallas_call x1, Pallas kernels, pack(): pl.pallas_call(partial(pack_kernel, tiles), grid=(2,), in_specs=[pl.Block...  9.35 us
    pallas_call x1, Pallas kernels, curvatures(): pl.pallas_call(partial(curvature_kernel, len(states)), grid=(blocks,), in...  5.14 us
    ppermute x1, waiting for transfers between devices, local(): bottom = lax.ppermute(cells[0], 'y', upward)  4.74 us
  transfers between devices with their start and end apart: 9, of which 6 were waited for; matrix products, arithmetic and copies ran while one was open for 0% of the time, Pallas kernels for 4%

commit v1 on v0

--- a/solution.py
+++ b/solution.py
@@ -185,10 +185,8 @@
     )(me, *pieces)
 
 
-def forecast_kernel(
-    inside, cells, top, bottom, force, out, now, later, push, turned, stage, done
-):
-    depth, span = now.shape[:2]
+def load_strip(source, strip, force, now, push, turned):
+    span = now.shape[1]
     lane = lane_index(LANES)
     unit = jnp.where(lax.broadcasted_iota(jnp.int32, lane.shape, 0) == lane, 1.0, 0.0).astype(BF16)
     line = lax.broadcasted_iota(jnp.int32, (8 * span, 2 * LANES), 0)
@@ -197,74 +195,87 @@
     place = lax.broadcasted_iota(jnp.int32, line.shape, 1)
     spread = (lax.rem(place, LANES) == wanted) & (place // LANES == sub // 4)
     spread = jnp.where(spread, 1.0, 0.0).astype(BF16)
-
-    for strip in range(PLANE + 2):
-        if strip == 0:
-            source = top
-        elif strip == PLANE + 1:
-            source = bottom
-        else:
-            source = cells.at[strip - 1]
-        for h in range(2):
-            edge = source[4 * h : 4 * h + 4, ROWS].reshape(LANES, LANES)
-            turned[0, h * LANES : (h + 1) * LANES] = against_rows(unit, edge) * 0.05
-
-        def load(i, carry):
-            for k in range(4):
-                r = 4 * i + k
-                row = strip * ROWS + r
-                both = jnp.concatenate(
-                    [source[4 * h : 4 * h + 4, r].reshape(LANES, LANES) for h in range(2)], 1
+    for h in range(2):
+        edge = source[4 * h : 4 * h + 4, ROWS].reshape(LANES, LANES)
+        turned[0, h * LANES : (h + 1) * LANES] = against_rows(unit, edge) * 0.05
+
+    def load(i, carry):
+        for k in range(4):
+            r = 4 * i + k
+            row = strip * ROWS + r
+            both = jnp.concatenate(
+                [source[4 * h : 4 * h + 4, r].reshape(LANES, LANES) for h in range(2)], 1
+            )
+            main = against_rows(spread, both) * 0.05
+            for c in range(span):
+                now[row, c] = main[8 * c : 8 * c + 8]
+            at = pl.multiple_of(16 * r, 16)
+            for h in range(2):
+                for c in range(8):
+                    low = turned[0, pl.ds(h * LANES + at + c, 1)]
+                    high = turned[0, pl.ds(h * LANES + at + 8 + c, 1)]
+                    now[row, c, 4 * h : 4 * h + 1] = low
+                    now[row, span - 8 + c, 4 * h + 3 : 4 * h + 4] = high
+            pushes = force[pl.ds(pl.multiple_of(row * 8, 8), 8)]
+            for c in range(span):
+                push[row, c] = jnp.broadcast_to(pushes[:, c : c + 1], (8, LANES))
+        return carry
+
+    lax.fori_loop(0, ROWS // 4, load, 0)
+
+
+def advance(step, first, last, source, target, push):
+    low, high = step + 1, source.shape[1] - 2 - step
+
+    def pair(i, carry):
+        row = first + 2 * i
+        west = [source[row + k, low - 1] for k in range(2)]
+        here = [source[row + k, low] for k in range(2)]
+        for c in range(low, high + 1):
+            east = [source[row + k, c + 1] for k in range(2)]
+            column = [source[row - 1, c], *here, source[row + 2, c]]
+            for k in range(2):
+                above, below = column[k], column[k + 2]
+                turn = (west[k] - east[k]) + (above - below) + 0.05
+                target[row + k, c] = (
+                    push[row + k, c]
+                    + here[k] * turn
+                    + 0.05 * (east[k] + west[k])
+                    + 0.4 * (above + below)
                 )
-                main = against_rows(spread, both) * 0.05
-                for c in range(span):
-                    now[row, c] = main[8 * c : 8 * c + 8]
-                at = pl.multiple_of(16 * r, 16)
-                for h in range(2):
-                    for c in range(8):
-                        low = turned[0, pl.ds(h * LANES + at + c, 1)]
-                        high = turned[0, pl.ds(h * LANES + at + 8 + c, 1)]
-                        now[row, c, 4 * h : 4 * h + 1] = low
-                        now[row, span - 8 + c, 4 * h + 3 : 4 * h + 4] = high
-                pushes = force[pl.ds(pl.multiple_of(row * 8, 8), 8)]
-                for c in range(span):
-                    push[row, c] = jnp.broadcast_to(pushes[:, c : c + 1], (8, LANES))
-            return carry
-
-        lax.fori_loop(0, ROWS // 4, load, 0)
-
+            west, here = here, east
+        return carry
+
+    lax.fori_loop(0, (last + 1 - first) // 2, pair, 0)
+
+
+def inner_kernel(cells, force, now, later, push, turned):
+    for strip in range(PLANE):
+        load_strip(cells.at[strip], strip + 1, force, now, push, turned)
+    depth = now.shape[0]
+    fields = (now, later)
+    for step in range(STEPS):
+        first = ROWS + 1 + step
+        advance(step, first, depth - 1 - first, fields[step % 2], fields[1 - step % 2], push)
+
+
+def outer_kernel(inside, top, bottom, force, *refs):
+    out, now, later, push, turned = refs[3:]
+    depth, span = now.shape[:2]
+    load_strip(top, 0, force, now, push, turned)
+    load_strip(bottom, PLANE + 1, force, now, push, turned)
     keep_top, keep_bottom = inside[0], inside[1]
-    source, target = now, later
+    fields = (now, later)
     for step in range(STEPS):
-        low, high = step + 1, span - 2 - step
-
-        def pair(i, carry, source=source, target=target, low=low, high=high):
-            row = low + 2 * i
-            west = [source[row + k, low - 1] for k in range(2)]
-            here = [source[row + k, low] for k in range(2)]
-            for c in range(low, high + 1):
-                east = [source[row + k, c + 1] for k in range(2)]
-                column = [source[row - 1, c], *here, source[row + 2, c]]
-                for k in range(2):
-                    above, below = column[k], column[k + 2]
-                    turn = (west[k] - east[k]) + (above - below) + 0.05
-                    target[row + k, c] = (
-                        push[row + k, c]
-                        + here[k] * turn
-                        + 0.05 * (east[k] + west[k])
-                        + 0.4 * (above + below)
-                    )
-                west, here = here, east
-            return carry
-
-        lax.fori_loop(0, (depth - 2 - 2 * step) // 2, pair, 0)
+        source, target = fields[step % 2], fields[1 - step % 2]
+        first, last = step + 1, ROWS + step
+        advance(step, first, last, source, target, push)
+        advance(step, depth - 1 - last, depth - 1 - first, source, target, push)
         if step < STEPS - 1:
-            for c in range(low, high + 1):
+            for c in range(step + 1, span - 1 - step):
                 target[ROWS - 1, c] = target[ROWS - 1, c] * keep_top
                 target[depth - ROWS, c] = target[depth - ROWS, c] * keep_bottom
-        source, target = target, source
-
-    copies = []
+    source = fields[STEPS % 2]
     for strip in range(PLANE):
 
         def save(i, carry):
@@ -281,35 +292,39 @@
                         for c in range(4)
                     ]
                     part = slice(h * LANES, (h + 1) * LANES)
-                    stage[strip, part, pl.ds(at, LANES)] = jnp.concatenate(columns, 0).T
+                    out[strip, part, pl.ds(at, LANES)] = jnp.concatenate(columns, 0).T
             return carry
 
         lax.fori_loop(0, ROWS // 2, save, 0)
-        copies.append(pltpu.make_async_copy(stage.at[strip], out.at[strip], done.at[strip]))
-        copies[-1].start()
-    for copy in copies:
-        copy.wait()
-
-
-def forecast(inside, cells, top, bottom, force):
-    field = pltpu.VMEM(((PLANE + 2) * ROWS, 48, 8, LANES), F32)
+
+
+def forecast_inner(cells, force):
+    field = ((PLANE + 2) * ROWS, 48, 8, LANES)
     vmem = pl.BlockSpec(memory_space=pltpu.VMEM)
     return pl.pallas_call(
-        forecast_kernel,
-        in_specs=[pl.BlockSpec(memory_space=pltpu.SMEM), vmem, vmem, vmem, vmem],
-        out_specs=pl.BlockSpec(memory_space=pl.ANY),
-        out_shape=jax.ShapeDtypeStruct((PLANE, 2 * LANES, ROWS * LANES), F32),
-        scratch_shapes=[
-            field,
-            field,
-            field,
-            pltpu.VMEM((2, 2 * LANES, LANES), F32),
-            pltpu.VMEM((PLANE, 2 * LANES, ROWS * LANES), F32),
-            pltpu.SemaphoreType.DMA((PLANE,)),
-        ],
-        name="forecast",
-        compiler_params=pltpu.CompilerParams(vmem_limit_bytes=42 << 20),
-    )(inside, cells, top, bottom, force)
+        inner_kernel,
+        in_specs=[vmem, vmem],
+        out_specs=[vmem] * 3,
+        out_shape=[jax.ShapeDtypeStruct(field, F32)] * 3,
+        scratch_shapes=[pltpu.VMEM((1, 2 * LANES, LANES), F32)],
+        name="forecast_inner",
+        compiler_params=pltpu.CompilerParams(vmem_limit_bytes=4 << 20),
+    )(cells, force)
+
+
+def forecast_outer(inside, top, bottom, force, *fields):
+    vmem = pl.BlockSpec(memory_space=pltpu.VMEM)
+    return pl.pallas_call(
+        outer_kernel,
+        in_specs=[pl.BlockSpec(memory_space=pltpu.SMEM)] + [vmem] * 6,
+        out_specs=[vmem] * 4,
+        out_shape=[jax.ShapeDtypeStruct((PLANE, 2 * LANES, ROWS * LANES), F32)]
+        + [jax.ShapeDtypeStruct(field.shape, F32) for field in fields],
+        input_output_aliases={4: 1, 5: 2, 6: 3},
+        scratch_shapes=[pltpu.VMEM((2, 2 * LANES, LANES), F32)],
+        name="forecast_outer",
+        compiler_params=pltpu.CompilerParams(vmem_limit_bytes=4 << 20),
+    )(inside, top, bottom, force, *fields)[0]
 
 
 def curvature_kernel(pieces, *refs):
@@ -585,7 +600,8 @@
     cells = chunk.reshape(PLANE, groups, ROWS + 1, members, LANES)
     bottom = lax.ppermute(cells[0], "y", upward)
     top = lax.ppermute(cells[PLANE - 1], "y", downward)
-    states = (forecast(inside, cells, top, bottom, force),)
+    fields = forecast_inner(cells, force)
+    states = (forecast_outer(inside, top, bottom, force, *fields),)
     own, up, down = curvatures(states, extra)
     from_below = lax.ppermute(up, "y", upward)
     from_above = lax.ppermute(down, "y", downward)

time: 166 us -> 160 us (0.964)
  waiting for transfers between devices: 42.4 us -> 38.2 us
    ppermute x1, waiting for transfers between devices: 4.74 us -> 0.01 us  [local(): bottom = lax.ppermute(cells[0], 'y', upward)]
    pallas_call x1 -> x2, Pallas kernels: 30.1 us -> 29.9 us  [the longest x1 16.4 us: forecast_inner(): pl.pallas_call(inner_kernel, in_specs=[vmem, vmem], out_specs=[vmem] * 3,...]
  transfers between devices with their start and end apart: 9 -> 9, of which waited for: 6 -> 4; matrix products, arithmetic and copies ran while one was open for 0% -> 0% of each run, Pallas kernels for 4% -> 15%
where the time goes in v1:
time: 160 us
  Pallas kernels  64.4 us (40%)
  waiting for transfers between devices  38.2 us (24%)
  blocking collectives  34.6 us (22%)
  starting transfers between devices  22 us (14%)
    all_to_all x1, blocking collectives, local(): back = lax.all_to_all(sent, axes, 0, 0, tiled=True).reshape(analysed.shape)  34.6 us
    all_to_all x1, waiting for transfers between devices, local(): chunk = lax.all_to_all(chunk, axes, 0, 0, tiled=True)  31.4 us
    pallas_call x1, Pallas kernels, forecast_inner(): pl.pallas_call(inner_kernel, in_specs=[vmem, vmem], out_specs=[vmem] * 3,...  16.4 us
    pallas_call x1, Pallas kernels, forecast_outer(): pl.pallas_call(outer_kernel, in_specs=[pl.BlockSpec(memory_space=pltpu.SM...  13.5 us
    pallas_call x2, Pallas kernels, transforms(): pl.pallas_call(partial(transform_kernel, bool(halo)), out_shape=jax.Shape...  11.4 us
    pallas_call x1, Pallas kernels, pack(): pl.pallas_call(partial(pack_kernel, tiles), grid=(2,), in_specs=[pl.Block...  9.44 us
    all_to_all x1, starting transfers between devices, local(): chunk = lax.all_to_all(chunk, axes, 0, 0, tiled=True)  9.42 us
    pallas_call x1, Pallas kernels, curvatures(): pl.pallas_call(partial(curvature_kernel, len(states)), grid=(blocks,), in...  5.15 us
  transfers between devices with their start and end apart: 9, of which 4 were waited for; matrix products, arithmetic and copies ran while one was open for 0% of the time, Pallas kernels for 15%

profile of v1, /device:TPU:1, one launch (start us, length us, event | category | flops | bytes accessed | tf_op | source)
XLA Modules:
  0.0 159.8 jit_solution(1324649350957016491)
XLA Ops:
  0.0 0.0 copy-start
  0.0 0.0 copy-start.1
  0.0 0.0 copy-start.2
  0.0 0.0 copy-start.3
  0.0 9.4 %pack.1 = bf16[32,9,32,128]{3,2,1,0:T(8,128)(2,1)} custom-call(f32[256,4096]{1,0:T(8,128)} %bitcast.28), custom_call_target="tpu_custom_call" | custom-call | tf_op jit(solution)/shard_map/pack/pallas_call | solution.py:137
  9.5 9.4 %all-to-all-start = ((bf16[32,9,32,128]{3,2,1,0:T(8,128)(2,1)}), bf16[32,9,32,128]{3,2,1,0:T(8,128)(2,1)S(1)}, u32[]{:S(2)}, u32[]{:S(2)}) async-start(bf16[32,9,32,128]{3,2,1,0:T(8,128)(2,1)} %pack.1), calls=%async_computation | async-start | bytes 4718592 | tf_op jit(solution)/shard_map/all_to_all | solution.py:599
  18.9 0.1 pad_add_fusion.me_ref
  19.0 0.0 copy-done
  19.0 0.0 copy-done.1
  19.0 0.0 copy-done.2
  19.0 0.0 copy-done.3
  19.0 0.7 pack_extra.1
  19.7 0.7 collective-permute-start.2
  20.4 0.1 add_convert_fusion.inside
  20.5 31.4 %all-to-all-done = bf16[32,9,32,128]{3,2,1,0:T(8,128)(2,1)S(1)} async-done(((bf16[32,9,32,128]{3,2,1,0:T(8,128)(2,1)}), bf16[32,9,32,128]{3,2,1,0:T(8,128)(2,1)S(1)}, u32[]{:S(2)}, u32[]{:S(2)}) %all-to-all-start) | async-done | bytes 2359328 | tf_op jit(solution)/shard_map/all_to_all | solution.py:599
  51.9 0.2 fusion
  52.1 1.3 collective-permute-start.1
  53.4 4.0 %collective-permute-start = (bf16[8,9,32,128]{3,2,1,0:T(8,128)(2,1)S(1)}, bf16[8,9,32,128]{3,2,1,0:T(8,128)(2,1)S(1)}, u32[]{:S(2)}, u32[]{:S(2)}) collective-permute-start(bf16[8,9,32,128]{3,2,1,0:T(8,128)(2,1)S(1)} %get-tuple-element.28), channel_id=1, source_target_pairs={{0,4},{4,8},{8,12},{1,5},{5,9},{9,13},{2,6},{6,10},{10,14},{3,7},{... | collective-permute-start | bytes 1769480 | tf_op jit(solution)/shard_map/ppermute | solution.py:602
  57.4 0.0 collective-permute-done.2
  57.5 0.3 collective-permute-start.3
  57.8 1.6 %collective-permute-start.4 = (f32[16,1024]{1,0:T(8,128)S(1)}, f32[16,1024]{1,0:T(8,128)S(1)}, u32[]{:S(2)}, u32[]{:S(2)}) collective-permute-start(f32[16,1024]{1,0:T(8,128)S(1)} %pad_maximum_fusion.2), channel_id=1, source_target_pairs={{0,2},{1,3},{2,0},{3,1},{4,6},{5,7},{6,4},{7,5},{8,10},{9,11},{10,... | collective-permute-start | bytes 196616 | tf_op jit(solution)/shard_map/ppermute | solution.py:595
  59.4 0.0 collective-permute-start.5
  59.5 0.0 collective-permute-done.3.one
  59.5 3.3 %collective-permute-done.4.two = f32[16,1024]{1,0:T(8,128)S(1)} collective-permute-done((f32[16,1024]{1,0:T(8,128)S(1)}, f32[16,1024]{1,0:T(8,128)S(1)}, u32[]{:S(2)}, u32[]{:S(2)}) %collective-permute-start.4) | collective-permute-done | bytes 65568 | tf_op jit(solution)/shard_map/ppermute | solution.py:595
  62.8 0.7 collective-permute-done.5.three
  63.5 0.7 forcing.1
  64.2 16.4 %forecast_inner.1 = (f32[48,48,8,128]{3,2,1,0:T(8,128)S(1)}, f32[48,48,8,128]{3,2,1,0:T(8,128)S(1)}, f32[48,48,8,128]{3,2,1,0:T(8,128)S(1)}) custom-call(bf16[4,8,9,32,128]{4,3,2,1,0:T(8,128)(2,1)S(1)} %bitcast.25, f32[384,128]{1,0:T(8,128)S(1)} %get-tuple-element.18.force), custom_call_target="tpu_custom_call" | custom-call | tf_op jit(solution)/shard_map/forecast_inner/pallas_call | solution.py:304
  80.5 0.0 collective-permute-done.1.bottom
  80.5 0.0 collective-permute-done.top
  80.5 13.5 %forecast_outer.1 = (f32[4,256,1024]{2,1,0:T(8,128)S(1)}, f32[48,48,8,128]{3,2,1,0:T(8,128)S(1)}, f32[48,48,8,128]{3,2,1,0:T(8,128)S(1)}, f32[48,48,8,128]{3,2,1,0:T(8,128)S(1)}) custom-call(f32[2]{0:T(128)S(1)} %add_convert_fusion.inside, ...), custom_call_target="tpu_custom_call", output_to_operand_aliasing={{1}: (4, {}), {2}: (5, {}), {3}: (6, {})} | custom-call | tf_op jit(solution)/shard_map/forecast_outer/pallas_call | solution.py:317
  94.1 5.1 %curvature.1 = (f32[4,264,256]{2,1,0:T(8,128)S(1)}, f32[264,256]{1,0:T(8,128)S(1)}, f32[264,256]{1,0:T(8,128)S(1)}) custom-call(f32[4,256,1024]{2,1,0:T(8,128)S(1)} %get-tuple-element.22.refs_0_, f32[4,8,1024]{2,1,0:T(8,128)S(1)} %get-tuple-element.23.refs_1_), custom_call_target="tpu_custom_call" | custom-call | tf_op jit(solution)/shard_map/curvature/pallas_call | solution.py:417
  99.2 3.2 %collective-permute-start.6 = (f32[264,256]{1,0:T(8,128)S(1)}, f32[264,256]{1,0:T(8,128)S(1)}, u32[]{:S(2)}, u32[]{:S(2)}) collective-permute-start(f32[264,256]{1,0:T(8,128)S(1)} %get-tuple-element.25), channel_id=1, source_target_pairs={{0,4},{4,8},{8,12},{1,5},{5,9},{9,13},{2,6},{6,10},{10,14},{3,7},{... | collective-permute-start | bytes 811016 | tf_op jit(solution)/shard_map/ppermute | solution.py:607
  102.4 1.5 collective-permute-start.7
  103.9 5.7 %transform.2.refs_1_ = f32[2,264,256]{2,1,0:T(8,128)S(1)} custom-call(f32[4,264,256]{2,1,0:T(8,128)S(1)} %get-tuple-element.24.refs_0_), custom_call_target="tpu_custom_call" | custom-call | tf_op jit(solution)/shard_map/transform/pallas_call | solution.py:485
  109.6 0.0 collective-permute-done.6.refs_1_
  109.6 2.8 %collective-permute-done.7.refs_2_ = f32[264,256]{1,0:T(8,128)S(1)} collective-permute-done((f32[264,256]{1,0:T(8,128)S(1)}, f32[264,256]{1,0:T(8,128)S(1)}, u32[]{:S(2)}, u32[]{:S(2)}) %collective-permute-start.7) | collective-permute-done | bytes 270368 | tf_op jit(solution)/shard_map/ppermute | solution.py:606
  112.4 5.7 %transform.3.refs_2_ = f32[2,264,256]{2,1,0:T(8,128)S(1)} custom-call(f32[4,264,256]{2,1,0:T(8,128)S(1)} %get-tuple-element.24.refs_0_, f32[264,256]{1,0:T(8,128)S(1)} %collective-permute-done.6.refs_1_, f32[264,256]{1,0:T(8,128)S(1)} %collective-permute-done.7.refs_2_), custom_call_target="tpu_custom_call" | custom-call | tf_op jit(solution)/shard_map/transform/pallas_call | solution.py:485
  118.1 2.9 %apply.1 = bf16[4,8,272,128]{3,2,1,0:T(8,128)(2,1)S(1)} custom-call(f32[4,256,1024]{2,1,0:T(8,128)S(1)} %get-tuple-element.22.refs_0_, f32[2,264,256]{2,1,0:T(8,128)S(1)} %transform.2.refs_1_, f32[2,264,256]{2,1,0:T(8,128)S(1)} %transform.3.refs_2_), custom_call_target="tpu_custom_call" | custom-call | tf_op jit(solution)/shard_map/apply/pallas_call | solution.py:524
  121.0 34.6 %all_to_all.10 = bf16[32,272,128]{2,1,0:T(8,128)(2,1)S(1)} all-to-all(bf16[32,272,128]{2,1,0:T(8,128)(2,1)S(1)} %bitcast.26), channel_id=1, replica_groups=mesh['member'=8,'y'=4,'zc'=4] {'zc','member'}, dimensions={0} | all-to-all | bytes 4456448 | tf_op jit(solution)/shard_map/all_to_all | solution.py:612
  155.6 4.2 %unpack.1 = f32[256,4096]{1,0:T(8,128)} custom-call(bf16[4,8,272,128]{3,2,1,0:T(8,128)(2,1)S(1)} %bitcast.27), custom_call_target="tpu_custom_call" | custom-call | tf_op jit(solution)/shard_map/unpack/pallas_call | solution.py:562
  (6 shorter events, 0.0 us)
Async XLA Ops:
  0.0 19.0 %copy-start = (f32[8,4096]{1,0:T(8,128)S(1)}, f32[8,4096]{1,0:T(8,128)}, u32[]{:S(2)}) copy-start(f32[8,4096]{1,0:T(8,128)} %drive) | copy-start | bytes 393220
  0.0 19.0 %copy-start.1 = (f32[1,4,1024]{2,1,0:T(4,128)S(1)}, f32[1,4,1024]{2,1,0:T(4,128)}, u32[]{:S(2)}) copy-start(f32[1,4,1024]{2,1,0:T(4,128)} %value.1) | copy-start | bytes 49156
  0.0 19.0 %copy-start.2 = (s32[1,4,1024]{2,1,0:T(4,128)S(1)}, s32[1,4,1024]{2,1,0:T(4,128)}, u32[]{:S(2)}) copy-start(s32[1,4,1024]{2,1,0:T(4,128)} %index.1) | copy-start | bytes 49156
  0.0 19.0 %copy-start.3 = (bf16[1,4,1024]{2,1,0:T(4,128)(2,1)S(1)}, bf16[1,4,1024]{2,1,0:T(4,128)(2,1)}, u32[]{:S(2)}) copy-start(bf16[1,4,1024]{2,1,0:T(4,128)(2,1)} %weight.1) | copy-start | bytes 24580
  9.5 42.4 %all-to-all-start = ((bf16[32,9,32,128]{3,2,1,0:T(8,128)(2,1)}), bf16[32,9,32,128]{3,2,1,0:T(8,128)(2,1)S(1)}, u32[]{:S(2)}, u32[]{:S(2)}) async-start(bf16[32,9,32,128]{3,2,1,0:T(8,128)(2,1)} %pack.1), calls=%async_computation | async-start | bytes 4718592 | tf_op jit(solution)/shard_map/all_to_all | solution.py:599
  19.7 37.7 %collective-permute-start.2 = (f32[4,8,1024]{2,1,0:T(8,128)S(1)}, f32[4,8,1024]{2,1,0:T(8,128)S(1)}, u32[]{:S(2)}, u32[]{:S(2)}) collective-permute-start(f32[4,8,1024]{2,1,0:T(8,128)S(1)} %pack_extra.1), channel_id=1, source_target_pairs={{4,0},{8,4},{12,8},{3,7},{7,11},{11,15},{20,16},{24,20},{28,24},{1... | collective-permute-start | bytes 393224 | tf_op jit(solution)/shard_map/ppermute | solution.py:592
  52.1 28.4 %collective-permute-start.1 = (bf16[8,9,32,128]{3,2,1,0:T(8,128)(2,1)S(1)}, bf16[8,9,32,128]{3,2,1,0:T(8,128)(2,1)S(1)}, u32[]{:S(2)}, u32[]{:S(2)}) collective-permute-start(bf16[8,9,32,128]{3,2,1,0:T(8,128)(2,1)S(1)} %get-tuple-element.27), channel_id=1, source_target_pairs={{4,0},{8,4},{12,8},{5,1},{9,5},{13,9},{6,2},{10,6},{14,10},{7,3},{... | collective-permute-start | bytes 1769480 | tf_op jit(solution)/shard_map/ppermute | solution.py:601
  53.4 27.1 %collective-permute-start = (bf16[8,9,32,128]{3,2,1,0:T(8,128)(2,1)S(1)}, bf16[8,9,32,128]{3,2,1,0:T(8,128)(2,1)S(1)}, u32[]{:S(2)}, u32[]{:S(2)}) collective-permute-start(bf16[8,9,32,128]{3,2,1,0:T(8,128)(2,1)S(1)} %get-tuple-element.28), channel_id=1, source_target_pairs={{0,4},{4,8},{8,12},{1,5},{5,9},{9,13},{2,6},{6,10},{10,14},{3,7},{... | collective-permute-start | bytes 1769480 | tf_op jit(solution)/shard_map/ppermute | solution.py:602
  57.5 2.0 %collective-permute-start.3 = (f32[16,1024]{1,0:T(8,128)S(1)}, f32[16,1024]{1,0:T(8,128)S(1)}, u32[]{:S(2)}, u32[]{:S(2)}) collective-permute-start(f32[16,1024]{1,0:T(8,128)S(1)} %pad_maximum_fusion.1), channel_id=1, source_target_pairs={{0,1},{1,2},{2,3},{3,0},{4,5},{5,6},{6,7},{7,4},{8,9},{9,10},{10,1... | collective-permute-start | bytes 196616 | tf_op jit(solution)/shard_map/ppermute | solution.py:595
  57.8 5.0 %collective-permute-start.4 = (f32[16,1024]{1,0:T(8,128)S(1)}, f32[16,1024]{1,0:T(8,128)S(1)}, u32[]{:S(2)}, u32[]{:S(2)}) collective-permute-start(f32[16,1024]{1,0:T(8,128)S(1)} %pad_maximum_fusion.2), channel_id=1, source_target_pairs={{0,2},{1,3},{2,0},{3,1},{4,6},{5,7},{6,4},{7,5},{8,10},{9,11},{10,... | collective-permute-start | bytes 196616 | tf_op jit(solution)/shard_map/ppermute | solution.py:595
  59.4 4.0 %collective-permute-start.5 = (f32[16,1024]{1,0:T(8,128)S(1)}, f32[16,1024]{1,0:T(8,128)S(1)}, u32[]{:S(2)}, u32[]{:S(2)}) collective-permute-start(f32[16,1024]{1,0:T(8,128)S(1)} %pad_maximum_fusion.3), channel_id=1, source_target_pairs={{0,3},{1,0},{2,1},{3,2},{4,7},{5,4},{6,5},{7,6},{8,11},{9,8},{10,9... | collective-permute-start | bytes 196616 | tf_op jit(solution)/shard_map/ppermute | solution.py:595
  99.2 10.4 %collective-permute-start.6 = (f32[264,256]{1,0:T(8,128)S(1)}, f32[264,256]{1,0:T(8,128)S(1)}, u32[]{:S(2)}, u32[]{:S(2)}) collective-permute-start(f32[264,256]{1,0:T(8,128)S(1)} %get-tuple-element.25), channel_id=1, source_target_pairs={{0,4},{4,8},{8,12},{1,5},{5,9},{9,13},{2,6},{6,10},{10,14},{3,7},{... | collective-permute-start | bytes 811016 | tf_op jit(solution)/shard_map/ppermute | solution.py:607
  102.4 10.0 %collective-permute-start.7 = (f32[264,256]{1,0:T(8,128)S(1)}, f32[264,256]{1,0:T(8,128)S(1)}, u32[]{:S(2)}, u32[]{:S(2)}) collective-permute-start(f32[264,256]{1,0:T(8,128)S(1)} %get-tuple-element.26), channel_id=1, source_target_pairs={{4,0},{8,4},{12,8},{5,1},{9,5},{13,9},{6,2},{10,6},{14,10},{7,3},{... | collective-permute-start | bytes 811016 | tf_op jit(solution)/shard_map/ppermute | solution.py:606
